TPU v7x, 32 devices: a whole 2x2x4 slice. The times are simulated.
32 devices in a mesh: group: 2 (over x), wide: 16 (over z, y, core).
Axes of the slice: x: 2, y: 2, z: 4, core: 2. Of those that a mesh axis runs over, the one named last changes fastest.
Arguments:
- stream_index: int32 [2], P('group'), parts along dimension 0, may hold values from 0 to 16777215
- forcing: bfloat16 [32, 1536, 1536], P('group', 'wide'), parts along dimension 0, may hold values from -144 to 144
Outputs:
- pressure: bfloat16 [32, 1536, 1536], P('group', 'wide'), parts along dimension 0
There are 2 independent parts, one for each index of `group`. A program takes and returns all parts, laid end to end along the dimension named above; each array names one. Nothing has to cross between parts.
All inputs are finite; a program needn't handle non-finite values.
Results may differ from a plain program's by a relative error of at most 0.0045.
Values may be sent and summed in bfloat16 or wider, within the bound.
No kernel may reach another device: no remote copies, remote signals or barrier semaphores. Data moves between devices by JAX's collectives and lax.ppermute only.
A program may use at most 192 MiB of HBM per device.

v0:
```python
import math
import jax
import jax.numpy as jnp
from jax import lax
from jax.sharding import PartitionSpec as P

LEN_X = 1536
LEN_Y = 1536
ITERS = 4


def with_halo(block, sides, width):
    for axis, dim in sides:
        count = lax.axis_size(axis)
        forward = [(i, i + 1) for i in range(count - 1)]
        backward = [(target, source) for source, target in forward]
        low = lax.ppermute(
            lax.slice_in_dim(block, block.shape[dim] - width, None, axis=dim), axis, forward
        )
        high = lax.ppermute(lax.slice_in_dim(block, 0, width, axis=dim), axis, backward)
        block = jnp.concatenate([low, block, high], axis=dim)
    return block


def scramble(value):
    value = value ^ value >> 16 & 65535
    value = value * 73244475
    value = value ^ value >> 16 & 65535
    value = value * 73244475
    value = value ^ value >> 16 & 65535
    return value


def cosine_basis(length):
    row_idx = lax.broadcasted_iota(jnp.int32, (length, length), 0)
    mode_idx = lax.broadcasted_iota(jnp.int32, (length, length), 1)
    phase = (2 * row_idx + 1) * mode_idx % (4 * length)
    angle = phase.astype(jnp.float32) * (math.pi / (2.0 * length))
    weights = jnp.where(mode_idx == 0, math.sqrt(1.0 / length), math.sqrt(2.0 / length))
    return (weights * jnp.cos(angle)).astype(jnp.bfloat16)


def coefficient_plane(stream_key, mode_z, depth):
    mode_x = lax.broadcasted_iota(jnp.int32, (LEN_X, LEN_Y), 0)
    mode_y = lax.broadcasted_iota(jnp.int32, (LEN_X, LEN_Y), 1)
    counter = (mode_z * LEN_X + mode_x) * LEN_Y + mode_y
    bits_a = scramble(2 * counter ^ stream_key)
    bits_b = scramble(2 * counter + 1 ^ stream_key)
    uniform_a = (bits_a >> 8 & 16777215).astype(jnp.float32) * 2.0 ** (-24) + 2.0 ** (-25)
    uniform_b = (bits_b >> 8 & 16777215).astype(jnp.float32) * 2.0 ** (-24) + 2.0 ** (-25)
    noise = jnp.sqrt(-2.0 * jnp.log(uniform_a)) * jnp.cos(2.0 * math.pi * uniform_b)
    freq_x = mode_x.astype(jnp.float32) * (math.pi / LEN_X)
    freq_y = mode_y.astype(jnp.float32) * (math.pi / LEN_Y)
    freq_z = mode_z.astype(jnp.float32) * (math.pi / depth)
    amplitude = 1.0 / jnp.sqrt(0.05 + freq_x * freq_x + freq_y * freq_y + freq_z * freq_z)
    return (amplitude * noise).astype(jnp.bfloat16)


def contract_last(left, table):
    return lax.dot_general(
        left, table, (((left.ndim - 1,), (1,)), ((), ())), preferred_element_type=jnp.float32
    )


def operate(wide_p, wide_k):
    center_p = wide_p[:, 1:-1]
    center_k = wide_k[:, 1:-1]
    total = 0.5 * (center_k + wide_k[:, 2:]) * (center_p - wide_p[:, 2:])
    total = total + 0.5 * (center_k + wide_k[:, :-2]) * (center_p - wide_p[:, :-2])
    for axis in (0, 2):
        widths = [(0, 0), (0, 0), (0, 0)]
        widths[axis] = (1, 1)
        padded_p = jnp.pad(center_p, widths)
        padded_k = jnp.pad(center_k, widths)
        size_here = center_p.shape[axis]
        for start in (0, 2):
            near_p = lax.slice_in_dim(padded_p, start, start + size_here, axis=axis)
            near_k = lax.slice_in_dim(padded_k, start, start + size_here, axis=axis)
            total = total + 0.5 * (center_k + near_k) * (center_p - near_p)
    return total


def body(stream_index, forcing):
    depth = forcing.shape[0]
    planes_here = depth // lax.axis_size("wide")
    stream_key = scramble(stream_index[0] ^ 1540483477)
    basis_x = cosine_basis(LEN_X)
    basis_y = cosine_basis(LEN_Y)
    basis_z = cosine_basis(depth)
    first_mode = lax.axis_index("wide") * planes_here
    own_modes = first_mode + jnp.arange(planes_here, dtype=jnp.int32)

    def rows_for(mode_z):
        coeff = coefficient_plane(stream_key, mode_z, depth)
        return jnp.dot(basis_x, coeff, preferred_element_type=jnp.float32).astype(jnp.bfloat16)

    def both_axes(mode_z):
        return contract_last(rows_for(mode_z), basis_y).astype(jnp.bfloat16)

    planes = lax.map(both_axes, own_modes)
    block = lax.all_to_all(planes, "wide", split_axis=1, concat_axis=0, tiled=True)
    count_z, count_x, count_y = block.shape
    field = jnp.dot(
        basis_z, block.reshape(count_z, count_x * count_y), preferred_element_type=jnp.float32
    )
    field = field.reshape(count_z, count_x, count_y)
    perm = jnp.exp(1.5 * jnp.tanh(2.0 * field))
    source = forcing.astype(jnp.float32)
    theta = 27.9
    delta = 26.1
    sigma = theta / delta
    rho = 1.0 / sigma
    step = source / theta
    press = step
    perm_wide = with_halo(perm.astype(jnp.bfloat16), (("wide", 1),), 1).astype(perm.dtype)
    for count in range(ITERS - 1):
        press_wide = with_halo(press, (("wide", 1),), 1)
        resid = source - operate(press_wide, perm_wide)
        rho_next = 1.0 / (2.0 * sigma - rho)
        step = rho_next * rho * step + 2.0 * rho_next / delta * resid
        press = press + step
        rho = rho_next
    return press.astype(jnp.bfloat16)


def solution(mesh):
    return jax.shard_map(
        body,
        mesh=mesh,
        in_specs=(P("group"), P("group", "wide", None)),
        out_specs=P("group", "wide", None),
        check_vma=False,
    )
```

profile of v0, /device:TPU:18, one launch (start us, length us, event | category | flops | bytes accessed | tf_op | source)
XLA Modules:
  0.0 644.1 jit_solution(15394397886811121742)
XLA Ops:
  0.7 36.9 %fusion.145 = bf16[1536,1536]{1,0:T(8,128)(2,1)S(1)} fusion(s32[1536]{0:T(1024)S(1)} %get-tuple-element.48, f32[1536]{0:T(1024)S(1)} %get-tuple-element.50), kind=kLoop, calls=%fused_computation.60.clone.clone.1 | loop fusion | flops 25952256 | bytes 4730880 | tf_op jit(solution)/shard_map/while/body/eval_jaxpr/dot_general | solution.py:60
  37.6 45.8 %multiply_convert_fusion.5 = bf16[1536,1536]{1,0:T(8,128)(2,1)S(1)} fusion(s32[]{:T(128)S(6)} %xor.65, s32[1536]{0:T(1024)S(1)} %get-tuple-element.47, f32[]{:T(128)S(6)} %mul.293, f32[1536]{0:T(1024)S(1)} %get-tuple-element.49, f32[1536]{0:T(1024)S(1)} %broadcast_add_fusion), kind=kLoop, calls=%fused_computation.101.clone.clone.2 | loop fusion | flops 103809024 | bytes 4737032 | tf_op jit(solution)/shard_map/while/body/eval_jaxpr/dot_general | solution.py:95
  83.4 42.3 %convolution_convert_fusion.1 = bf16[1536,1536]{1,0:T(8,128)(2,1)S(1)} fusion(s32[1536]{0:T(1024)S(1)} %get-tuple-element.48, f32[1536]{0:T(1024)S(1)} %get-tuple-element.50, bf16[1536,1536]{1,0:T(8,128)(2,1)S(1)} %multiply_convert_fusion.5), kind=kOutput, calls=%fused_computation.107 | convolution fusion | flops 7276068864 | bytes 9449472 | tf_op jit(solution)/shard_map/while/body/eval_jaxpr/dot_general | solution.py:95
  125.7 8.0 %fusion.71 = bf16[1,1536,1536]{2,1,0:T(8,128)(2,1)S(1)} fusion(bf16[1536,1536]{1,0:T(8,128)(2,1)S(1)} %convolution_convert_fusion.1, bf16[1536,1536]{1,0:T(8,128)(2,1)S(1)} %fusion.145), kind=kOutput, calls=%fused_computation.108 | convolution fusion | flops 7250116608 | bytes 14155776 | tf_op jit(solution)/shard_map/while/body/eval_jaxpr/dot_general | solution.py:60
  133.7 52.2 %copy.30 = bf16[1,1536,1536]{2,0,1:T(2,128)(2,1)} copy(bf16[1,1536,1536]{2,1,0:T(8,128)(2,1)S(1)} %fusion.71) | data formatting | bytes 9437184 | tf_op jit(solution)/shard_map/while/body/jit(dynamic_update_index_in_dim)/broadcast_in_dim | solution.py:100
  185.9 0.6 broadcast.337
  186.5 31.9 %reduce.2 = bf16[1536,1536]{1,0:T(8,128)(2,1)} reduce(bf16[1536,1,1536]{2,1,0:T(2,128)(2,1)} %bitcast.21, bf16[]{:T(256)} %broadcast.337), dimensions={1}, to_apply=%bitcast.20.reduce_sub_computation | reduce | bytes 9437186
  218.4 11.8 %reshape.15 = bf16[16,2,73728]{2,1,0:T(2,128)(2,1)} reshape(bf16[1536,1536]{1,0:T(8,128)(2,1)} %reduce.2) | data formatting | bytes 9437184
  230.2 6.7 %all-to-all-start = ((bf16[16,2,73728]{2,1,0:T(2,128)(2,1)}), bf16[16,2,73728]{2,1,0:T(2,128)(2,1)}, u32[]{:S(2)}, u32[]{:S(2)}) async-start(bf16[16,2,73728]{2,1,0:T(2,128)(2,1)} %reshape.15), calls=%async_computation | async-start | bytes 9437184 | tf_op jit(solution)/shard_map/all_to_all | solution.py:101
  237.0 9.6 %convert_multiply_fusion.1 = f32[16,96,1536]{2,0,1:T(8,128)} fusion(bf16[16,96,1536]{2,1,0:T(8,128)(2,1)} %param.3), kind=kLoop, calls=%fused_computation.4 | loop fusion | flops 4718592 | bytes 14155776 | tf_op jit(solution)/shard_map/div | solution.py:113
  246.6 94.1 %all-to-all-done = bf16[16,2,73728]{2,1,0:T(2,128)(2,1)} async-done(((bf16[16,2,73728]{2,1,0:T(2,128)(2,1)}), bf16[16,2,73728]{2,1,0:T(2,128)(2,1)}, u32[]{:S(2)}, u32[]{:S(2)}) %all-to-all-start) | async-done | bytes 4718624 | tf_op jit(solution)/shard_map/all_to_all | solution.py:101
  340.7 12.8 %reshape.16 = bf16[1536,1,1536]{2,1,0:T(2,128)(2,1)} reshape(bf16[16,2,73728]{2,1,0:T(2,128)(2,1)} %all-to-all-done) | data formatting | bytes 9437184
  353.5 31.3 %bitcast_reduce_fusion = bf16[1536,1536]{1,0:T(8,128)(2,1)} fusion(bf16[1536,1,1536]{2,1,0:T(2,128)(2,1)} %reshape.16), kind=kLoop, calls=%fused_computation.181 | loop fusion | bytes 9437184 | tf_op jit(solution)/shard_map/all_to_all | solution.py:101
  384.9 5.2 reshape.12
  390.1 5.1 exponential_convert_fusion
  395.2 1.9 collective-permute-start
  397.1 4.5 collective-permute-start.1
  401.6 1.0 fusion.135
  402.6 1.9 collective-permute-start.2
  404.5 2.6 collective-permute-start.3
  407.1 0.0 collective-permute-done
  407.1 0.0 collective-permute-done.1
  407.1 0.7 maximum_convert_fusion
  407.9 0.0 copy-start
  407.9 5.0 slice.154
  412.9 1.7 copy-done
  414.7 0.0 collective-permute-done.2
  414.7 0.0 collective-permute-done.3
  414.7 59.3 %fusion = (f32[16,96,1536]{2,0,1:T(8,128)}, f32[16,96,1536]{2,0,1:T(8,128)}) fusion(bf16[16,96,1536]{2,1,0:T(8,128)(2,1)} %param.3, f32[16,96,1536]{2,0,1:T(8,128)} %slice.154, f32[16,96,1536]{2,0,1:T(8,128)} %convert_multiply_fusion.1, f32[16,1,1536]{2,0,1:T(8,128)S(1)} %collective-permute-done.3, f32[16,98,1536]{2,0,1:T(8,128)} %copy-done, ...), kind=kLoop, calls=%fused_computation.14 | loop fusion | flops 89653248 | bytes 70975488 | tf_op jit(solution)/shard_map/add | solution.py:121
  474.0 1.0 fusion.134
  475.0 4.1 collective-permute-start.4
  479.0 1.9 collective-permute-start.5
  481.0 0.3 collective-permute-done.4
  481.2 4.6 collective-permute-done.5
  485.9 69.9 %fusion.92 = (f32[16,96,1536]{2,0,1:T(8,128)}, f32[16,96,1536]{2,0,1:T(8,128)}) fusion(f32[16,96,1536]{2,0,1:T(8,128)} %get-tuple-element.38, bf16[16,96,1536]{2,1,0:T(8,128)(2,1)} %param.3, f32[16,96,1536]{2,0,1:T(8,128)} %get-tuple-element.37, f32[16,96,1536]{2,0,1:T(8,128)} %slice.154, f32[16,1,1536]{2,0,1:T(8,128)S(1)} %collective-permute-done.5, ...), kind=kLoop, calls=%fused_computation.128 | loop fusion | flops 92012544 | bytes 80412672 | tf_op jit(solution)/shard_map/add | solution.py:121
  555.7 1.0 fusion.133
  556.7 1.9 collective-permute-start.6
  558.6 2.6 collective-permute-start.7
  561.2 0.0 collective-permute-done.6
  561.3 4.2 collective-permute-done.7
  565.5 71.4 %add_convert_fusion = bf16[16,96,1536]{2,0,1:T(8,128)(2,1)} fusion(f32[16,96,1536]{2,0,1:T(8,128)} %get-tuple-element.35, f32[16,96,1536]{2,0,1:T(8,128)} %get-tuple-element.36, f32[16,1,1536]{2,0,1:T(8,128)S(1)} %collective-permute-done.7, f32[16,1,1536]{2,0,1:T(8,128)S(1)} %collective-permute-done.6, bf16[16,96,1536]{2,1,0:T(8,128)(2,1)} %param.3, ...), kind=kLoop, calls=%fused_computation.98 | loop fusion | flops 89653248 | bytes 66256896 | tf_op jit(solution)/shard_map/convert_element_type | solution.py:123
  636.8 7.1 %copy.15 = bf16[16,96,1536]{2,1,0:T(8,128)(2,1)} copy(bf16[16,96,1536]{2,0,1:T(8,128)(2,1)} %add_convert_fusion) | data formatting | bytes 9437184 | tf_op jit(solution)/shard_map/convert_element_type | solution.py:123
  (6 shorter events, 0.0 us)
Async XLA Ops:
  230.2 110.5 %all-to-all-start = ((bf16[16,2,73728]{2,1,0:T(2,128)(2,1)}), bf16[16,2,73728]{2,1,0:T(2,128)(2,1)}, u32[]{:S(2)}, u32[]{:S(2)}) async-start(bf16[16,2,73728]{2,1,0:T(2,128)(2,1)} %reshape.15), calls=%async_computation | async-start | bytes 9437184 | tf_op jit(solution)/shard_map/all_to_all | solution.py:101
  395.2 12.0 %collective-permute-start = (bf16[16,1,1536]{2,0,1:T(8,128)(2,1)S(1)}, bf16[16,1,1536]{2,0,1:T(8,128)(2,1)S(1)}, u32[]{:S(2)}, u32[]{:S(2)}) collective-permute-start(bf16[16,1,1536]{2,0,1:T(8,128)(2,1)S(1)} %get-tuple-element.45), channel_id=1, source_target_pairs={{0,1},{1,2},{2,3},{3,4},{4,5},{5,6},{6,7},{7,8},{8,9},{9,10},{10,1... | collective-permute-start | bytes 147464 | tf_op jit(solution)/shard_map/ppermute | solution.py:17
  397.1 10.0 %collective-permute-start.1 = (bf16[16,1,1536]{2,0,1:T(8,128)(2,1)S(1)}, bf16[16,1,1536]{2,0,1:T(8,128)(2,1)S(1)}, u32[]{:S(2)}, u32[]{:S(2)}) collective-permute-start(bf16[16,1,1536]{2,0,1:T(8,128)(2,1)S(1)} %get-tuple-element.46), channel_id=1, source_target_pairs={{1,0},{2,1},{3,2},{4,3},{5,4},{6,5},{7,6},{8,7},{9,8},{10,9},{11,1... | collective-permute-start | bytes 147464 | tf_op jit(solution)/shard_map/ppermute | solution.py:20
  402.6 12.1 %collective-permute-start.2 = (f32[16,1,1536]{2,0,1:T(8,128)S(1)}, f32[16,1,1536]{2,0,1:T(8,128)S(1)}, u32[]{:S(2)}, u32[]{:S(2)}) collective-permute-start(f32[16,1,1536]{2,0,1:T(8,128)S(1)} %get-tuple-element.43), channel_id=1, source_target_pairs={{1,0},{2,1},{3,2},{4,3},{5,4},{6,5},{7,6},{8,7},{9,8},{10,9},{11,1... | collective-permute-start | bytes 294920 | tf_op jit(solution)/shard_map/ppermute | solution.py:20
  404.5 10.2 %collective-permute-start.3 = (f32[16,1,1536]{2,0,1:T(8,128)S(1)}, f32[16,1,1536]{2,0,1:T(8,128)S(1)}, u32[]{:S(2)}, u32[]{:S(2)}) collective-permute-start(f32[16,1,1536]{2,0,1:T(8,128)S(1)} %get-tuple-element.44), channel_id=1, source_target_pairs={{0,1},{1,2},{2,3},{3,4},{4,5},{5,6},{6,7},{7,8},{8,9},{9,10},{10,1... | collective-permute-start | bytes 294920 | tf_op jit(solution)/shard_map/ppermute | solution.py:17
  407.9 6.8 %copy-start = (f32[16,98,1536]{2,0,1:T(8,128)}, f32[16,98,1536]{2,0,1:T(8,128)S(1)}, u32[]{:S(2)}) copy-start(f32[16,98,1536]{2,0,1:T(8,128)S(1)} %maximum_convert_fusion) | copy-start | bytes 28901380
  475.0 6.3 collective-permute-start.4
  479.0 6.8 %collective-permute-start.5 = (f32[16,1,1536]{2,0,1:T(8,128)S(1)}, f32[16,1,1536]{2,0,1:T(8,128)S(1)}, u32[]{:S(2)}, u32[]{:S(2)}) collective-permute-start(f32[16,1,1536]{2,0,1:T(8,128)S(1)} %get-tuple-element.42), channel_id=1, source_target_pairs={{0,1},{1,2},{2,3},{3,4},{4,5},{5,6},{6,7},{7,8},{8,9},{9,10},{10,1... | collective-permute-start | bytes 294920 | tf_op jit(solution)/shard_map/ppermute | solution.py:17
  556.7 4.6 collective-permute-start.6
  558.6 6.8 %collective-permute-start.7 = (f32[16,1,1536]{2,0,1:T(8,128)S(1)}, f32[16,1,1536]{2,0,1:T(8,128)S(1)}, u32[]{:S(2)}, u32[]{:S(2)}) collective-permute-start(f32[16,1,1536]{2,0,1:T(8,128)S(1)} %get-tuple-element.40), channel_id=1, source_target_pairs={{0,1},{1,2},{2,3},{3,4},{4,5},{5,6},{6,7},{7,8},{8,9},{9,10},{10,1... | collective-permute-start | bytes 294920 | tf_op jit(solution)/shard_map/ppermute | solution.py:17
where the time goes:
time: 651 us; the launch traced here: 644 us
  other arithmetic  326 us (50%)
  local copies, waits for them, and re-layouts  131 us (20%)
  waiting for transfers between devices  103 us (16%)
  matrix products  55.3 us (8%)
  starting transfers between devices  28.2 us (4%)
    add x2, other arithmetic, body(): press = press + step  129 us
    all_to_all x1, waiting for transfers between devices, body(): lax.all_to_all(planes, 'wide', split_axis=1, concat_axis=0, tiled=True)  94.1 us
    convert_element_type x1, other arithmetic, body(): return press.astype(jnp.bfloat16)  71.4 us
    broadcast_in_dim x1, local copies, waits for them, and re-layouts, body(): planes = lax.map(both_axes, own_modes)  52.2 us
    dot_general x1, other arithmetic, rows_for(): jnp.dot(basis_x, coeff, preferred_element_type=jnp.float32)  45.8 us
    dot_general x1, matrix products, rows_for(): jnp.dot(basis_x, coeff, preferred_element_type=jnp.float32)  42.3 us
    dot_general x1, other arithmetic, contract_last(): lax.dot_general(left, table, (((left.ndim - 1,), (1,)), ((), ())), prefer...  36.9 us
    unnamed x1, other arithmetic  31.9 us
  transfers between devices with their start and end apart: 9, of which 4 were waited for; matrix products, arithmetic and copies ran while one was open for 3% of the time, Pallas kernels for 0%

commit v1 on v0

--- a/solution.py
+++ b/solution.py
@@ -98,7 +98,16 @@
         return contract_last(rows_for(mode_z), basis_y).astype(jnp.bfloat16)
 
     planes = lax.map(both_axes, own_modes)
-    block = lax.all_to_all(planes, "wide", split_axis=1, concat_axis=0, tiled=True)
+
+    def arrange_the_limits(in_array):
+        return jnp.concatenate(
+            jax.lax.all_to_all(
+                jnp.stack(jnp.split(in_array, jax.lax.psum(1, "wide"), axis=1)), "wide", 0, 0
+            ),
+            axis=0,
+        )
+
+    block = arrange_the_limits(planes)
     count_z, count_x, count_y = block.shape
     field = jnp.dot(
         basis_z, block.reshape(count_z, count_x * count_y), preferred_element_type=jnp.float32

time: 651 us -> 520 us (0.80)
  local copies, waits for them, and re-layouts: 131 us -> 28.2 us
  other arithmetic: 326 us -> 294 us
    broadcast_in_dim x1 -> x0, local copies, waits for them, and re-layouts: 52.2 us -> none  [body(): planes = lax.map(both_axes, own_modes)]
    unnamed x1 -> x0, other arithmetic: 31.9 us -> none
    all_to_all x1 -> x0, local copies, waits for them, and re-layouts: 31.3 us -> none  [body(): lax.all_to_all(planes, 'wide', split_axis=1, concat_axis=0, tiled=True)]
    unnamed x5 -> x17, local copies, waits for them, and re-layouts: 26.9 us -> 12.5 us
where the time goes in v1:
time: 520 us; the launch traced here: 513 us
  other arithmetic  294 us (57%)
  waiting for transfers between devices  103 us (20%)
  matrix products  58.5 us (11%)
  local copies, waits for them, and re-layouts  28.2 us (5%)
  starting transfers between devices  28.2 us (5%)
    add x2, other arithmetic, body(): press = press + step  130 us
    all_to_all x1, waiting for transfers between devices, arrange_the_limits(): jax.lax.all_to_all(jnp.stack(jnp.split(in_array, jax.lax.psum(1, 'wide'),...  94.1 us
    convert_element_type x1, other arithmetic, body(): return press.astype(jnp.bfloat16)  71.3 us
    dot_general x1, other arithmetic, rows_for(): jnp.dot(basis_x, coeff, preferred_element_type=jnp.float32)  45.8 us
    dot_general x1, matrix products, rows_for(): jnp.dot(basis_x, coeff, preferred_element_type=jnp.float32)  42.3 us
    dot_general x1, other arithmetic, contract_last(): lax.dot_general(left, table, (((left.ndim - 1,), (1,)), ((), ())), prefer...  36.9 us
    unnamed x17, local copies, waits for them, and re-layouts  12.5 us
    ppermute x4, starting transfers between devices, with_halo(): lax.ppermute(lax.slice_in_dim(block, 0, width, axis=dim), axis, backward)  12.4 us
  transfers between devices with their start and end apart: 9, of which 4 were waited for; matrix products, arithmetic and copies ran while one was open for 3% of the time, Pallas kernels for 0%

profile of v1, /device:TPU:18, one launch (start us, length us, event | category | flops | bytes accessed | tf_op | source)
XLA Modules:
  0.0 513.5 jit_solution(8739326212134612380)
XLA Ops:
  0.7 36.9 %fusion.161 = bf16[1536,1536]{1,0:T(8,128)(2,1)S(1)} fusion(s32[1536]{0:T(1024)S(1)} %get-tuple-element.48, f32[1536]{0:T(1024)S(1)} %get-tuple-element.50), kind=kLoop, calls=%fused_computation.60.clone.clone.1 | loop fusion | flops 25952256 | bytes 4730880 | tf_op jit(solution)/shard_map/while/body/eval_jaxpr/dot_general | solution.py:60
  37.6 45.8 %multiply_convert_fusion.5 = bf16[1536,1536]{1,0:T(8,128)(2,1)S(1)} fusion(s32[]{:T(128)S(6)} %xor.65, s32[1536]{0:T(1024)S(1)} %get-tuple-element.47, f32[]{:T(128)S(6)} %mul.293, f32[1536]{0:T(1024)S(1)} %get-tuple-element.49, f32[1536]{0:T(1024)S(1)} %broadcast_add_fusion), kind=kLoop, calls=%fused_computation.101.clone.clone.2 | loop fusion | flops 103809024 | bytes 4737032 | tf_op jit(solution)/shard_map/while/body/eval_jaxpr/dot_general | solution.py:95
  83.4 42.3 %convolution_convert_fusion.1 = bf16[1536,1536]{1,0:T(8,128)(2,1)S(1)} fusion(s32[1536]{0:T(1024)S(1)} %get-tuple-element.48, f32[1536]{0:T(1024)S(1)} %get-tuple-element.50, bf16[1536,1536]{1,0:T(8,128)(2,1)S(1)} %multiply_convert_fusion.5), kind=kOutput, calls=%fused_computation.107 | convolution fusion | flops 7276068864 | bytes 9449472 | tf_op jit(solution)/shard_map/while/body/eval_jaxpr/dot_general | solution.py:95
  125.7 7.8 %fusion.71 = bf16[1,1536,1536]{2,1,0:T(8,128)(2,1)S(1)} fusion(bf16[1536,1536]{1,0:T(8,128)(2,1)S(1)} %convolution_convert_fusion.1, bf16[1536,1536]{1,0:T(8,128)(2,1)S(1)} %fusion.161), kind=kOutput, calls=%fused_computation.108 | convolution fusion | flops 7250116608 | bytes 14155776 | tf_op jit(solution)/shard_map/while/body/eval_jaxpr/dot_general | solution.py:60
  133.5 0.7 fusion.108
  134.2 0.7 fusion.107
  135.0 0.7 fusion.106
  135.7 0.7 fusion.105
  136.4 0.7 fusion.104
  137.2 0.7 fusion.103
  137.9 0.7 fusion.102
  138.6 0.7 fusion.101
  139.4 0.7 fusion.100
  140.1 0.7 fusion.99
  140.8 0.7 fusion.98
  141.6 0.7 fusion.97
  142.3 0.7 fusion.96
  143.0 0.7 fusion.95
  143.8 0.7 fusion.94
  144.5 0.7 fusion.93
  145.2 6.5 %all-to-all-start = ((bf16[16,1,96,1536]{3,2,1,0:T(8,128)(2,1)}), bf16[16,1,96,1536]{3,2,1,0:T(8,128)(2,1)}, u32[]{:S(2)}, u32[]{:S(2)}) async-start(bf16[16,1,96,1536]{3,2,1,0:T(8,128)(2,1)} %fusion.93), calls=%async_computation | async-start | bytes 9437184 | tf_op jit(solution)/shard_map/all_to_all | solution.py:104
  151.8 9.6 %convert_multiply_fusion.1 = f32[16,96,1536]{2,0,1:T(8,128)} fusion(bf16[16,96,1536]{2,1,0:T(8,128)(2,1)} %param.3), kind=kLoop, calls=%fused_computation.4 | loop fusion | flops 4718592 | bytes 14155776 | tf_op jit(solution)/shard_map/div | solution.py:122
  161.4 94.1 %all-to-all-done = bf16[16,1,96,1536]{3,2,1,0:T(8,128)(2,1)} async-done(((bf16[16,1,96,1536]{3,2,1,0:T(8,128)(2,1)}), bf16[16,1,96,1536]{3,2,1,0:T(8,128)(2,1)}, u32[]{:S(2)}, u32[]{:S(2)}) %all-to-all-start) | async-done | bytes 4718624 | tf_op jit(solution)/shard_map/all_to_all | solution.py:104
  255.5 8.4 %exponential_convert_fusion = bf16[16,96,1536]{2,0,1:T(8,128)(2,1)S(1)} fusion(s32[16]{0:T(128)S(1)} %multiply_add_fusion.2, f32[16]{0:T(128)S(1)} %compare_select_fusion, bf16[2,8,96,1536]{3,2,1,0:T(8,128)(2,1)} %bitcast.23), kind=kOutput, calls=%fused_computation.100 | convolution fusion | flops 82579456 | bytes 9437312 | tf_op jit(solution)/shard_map/dot_general | solution.py:112
  264.0 1.9 collective-permute-start
  265.9 4.5 collective-permute-start.1
  270.5 1.0 fusion.151
  271.4 1.9 collective-permute-start.2
  273.4 2.8 collective-permute-start.3
  276.2 0.0 collective-permute-done
  276.2 0.0 collective-permute-done.1
  276.2 0.7 maximum_convert_fusion
  277.0 4.9 slice.154
  281.9 1.5 copy-done
  283.4 0.0 collective-permute-done.3
  283.4 59.9 %fusion = (f32[16,96,1536]{2,0,1:T(8,128)}, f32[16,96,1536]{2,0,1:T(8,128)}) fusion(bf16[16,96,1536]{2,1,0:T(8,128)(2,1)} %param.3, f32[16,96,1536]{2,0,1:T(8,128)} %slice.154, f32[16,96,1536]{2,0,1:T(8,128)} %convert_multiply_fusion.1, f32[16,1,1536]{2,0,1:T(8,128)S(1)} %collective-permute-done.3, f32[16,98,1536]{2,0,1:T(8,128)} %copy-done, ...), kind=kLoop, calls=%fused_computation.14 | loop fusion | flops 89653248 | bytes 70975488 | tf_op jit(solution)/shard_map/add | solution.py:130
  343.4 1.0 fusion.150
  344.3 4.1 collective-permute-start.4
  348.4 1.9 collective-permute-start.5
  350.3 0.3 collective-permute-done.4
  350.6 4.6 collective-permute-done.5
  355.2 69.9 %fusion.92 = (f32[16,96,1536]{2,0,1:T(8,128)}, f32[16,96,1536]{2,0,1:T(8,128)}) fusion(f32[16,96,1536]{2,0,1:T(8,128)} %get-tuple-element.38, bf16[16,96,1536]{2,1,0:T(8,128)(2,1)} %param.3, f32[16,96,1536]{2,0,1:T(8,128)} %get-tuple-element.37, f32[16,96,1536]{2,0,1:T(8,128)} %slice.154, f32[16,1,1536]{2,0,1:T(8,128)S(1)} %collective-permute-done.5, ...), kind=kLoop, calls=%fused_computation.128 | loop fusion | flops 92012544 | bytes 80412672 | tf_op jit(solution)/shard_map/add | solution.py:130
  425.2 1.0 fusion.149
  426.1 1.9 collective-permute-start.6
  428.1 2.6 collective-permute-start.7
  430.7 4.2 collective-permute-done.7
  434.9 71.3 %add_convert_fusion = bf16[16,96,1536]{2,0,1:T(8,128)(2,1)} fusion(f32[16,96,1536]{2,0,1:T(8,128)} %get-tuple-element.35, f32[16,96,1536]{2,0,1:T(8,128)} %get-tuple-element.36, f32[16,1,1536]{2,0,1:T(8,128)S(1)} %collective-permute-done.7, f32[16,1,1536]{2,0,1:T(8,128)S(1)} %collective-permute-done.6, bf16[16,96,1536]{2,1,0:T(8,128)(2,1)} %param.3, ...), kind=kLoop, calls=%fused_computation.98 | loop fusion | flops 89653248 | bytes 66256896 | tf_op jit(solution)/shard_map/convert_element_type | solution.py:132
  506.2 7.1 %copy.7 = bf16[16,96,1536]{2,1,0:T(8,128)(2,1)} copy(bf16[16,96,1536]{2,0,1:T(8,128)(2,1)} %add_convert_fusion) | data formatting | bytes 9437184 | tf_op jit(solution)/shard_map/convert_element_type | solution.py:132
  (9 shorter events, 0.0 us)
Async XLA Ops:
  145.2 110.3 %all-to-all-start = ((bf16[16,1,96,1536]{3,2,1,0:T(8,128)(2,1)}), bf16[16,1,96,1536]{3,2,1,0:T(8,128)(2,1)}, u32[]{:S(2)}, u32[]{:S(2)}) async-start(bf16[16,1,96,1536]{3,2,1,0:T(8,128)(2,1)} %fusion.93), calls=%async_computation | async-start | bytes 9437184 | tf_op jit(solution)/shard_map/all_to_all | solution.py:104
  264.0 12.2 %collective-permute-start = (bf16[16,1,1536]{2,0,1:T(8,128)(2,1)S(1)}, bf16[16,1,1536]{2,0,1:T(8,128)(2,1)S(1)}, u32[]{:S(2)}, u32[]{:S(2)}) collective-permute-start(bf16[16,1,1536]{2,0,1:T(8,128)(2,1)S(1)} %get-tuple-element.45), channel_id=1, source_target_pairs={{0,1},{1,2},{2,3},{3,4},{4,5},{5,6},{6,7},{7,8},{8,9},{9,10},{10,1... | collective-permute-start | bytes 147464 | tf_op jit(solution)/shard_map/ppermute | solution.py:17
  265.9 10.3 %collective-permute-start.1 = (bf16[16,1,1536]{2,0,1:T(8,128)(2,1)S(1)}, bf16[16,1,1536]{2,0,1:T(8,128)(2,1)S(1)}, u32[]{:S(2)}, u32[]{:S(2)}) collective-permute-start(bf16[16,1,1536]{2,0,1:T(8,128)(2,1)S(1)} %get-tuple-element.46), channel_id=1, source_target_pairs={{1,0},{2,1},{3,2},{4,3},{5,4},{6,5},{7,6},{8,7},{9,8},{10,9},{11,1... | collective-permute-start | bytes 147464 | tf_op jit(solution)/shard_map/ppermute | solution.py:20
  271.4 12.0 %collective-permute-start.2 = (f32[16,1,1536]{2,0,1:T(8,128)S(1)}, f32[16,1,1536]{2,0,1:T(8,128)S(1)}, u32[]{:S(2)}, u32[]{:S(2)}) collective-permute-start(f32[16,1,1536]{2,0,1:T(8,128)S(1)} %get-tuple-element.43), channel_id=1, source_target_pairs={{1,0},{2,1},{3,2},{4,3},{5,4},{6,5},{7,6},{8,7},{9,8},{10,9},{11,1... | collective-permute-start | bytes 294920 | tf_op jit(solution)/shard_map/ppermute | solution.py:20
  273.4 10.1 %collective-permute-start.3 = (f32[16,1,1536]{2,0,1:T(8,128)S(1)}, f32[16,1,1536]{2,0,1:T(8,128)S(1)}, u32[]{:S(2)}, u32[]{:S(2)}) collective-permute-start(f32[16,1,1536]{2,0,1:T(8,128)S(1)} %get-tuple-element.44), channel_id=1, source_target_pairs={{0,1},{1,2},{2,3},{3,4},{4,5},{5,6},{6,7},{7,8},{8,9},{9,10},{10,1... | collective-permute-start | bytes 294920 | tf_op jit(solution)/shard_map/ppermute | solution.py:17
  277.0 6.5 %copy-start = (f32[16,98,1536]{2,0,1:T(8,128)}, f32[16,98,1536]{2,0,1:T(8,128)S(1)}, u32[]{:S(2)}) copy-start(f32[16,98,1536]{2,0,1:T(8,128)S(1)} %maximum_convert_fusion) | copy-start | bytes 28901380
  344.3 6.3 %collective-permute-start.4 = (f32[16,1,1536]{2,0,1:T(8,128)S(1)}, f32[16,1,1536]{2,0,1:T(8,128)S(1)}, u32[]{:S(2)}, u32[]{:S(2)}) collective-permute-start(f32[16,1,1536]{2,0,1:T(8,128)S(1)} %get-tuple-element.41), channel_id=1, source_target_pairs={{1,0},{2,1},{3,2},{4,3},{5,4},{6,5},{7,6},{8,7},{9,8},{10,9},{11,1... | collective-permute-start | bytes 294920 | tf_op jit(solution)/shard_map/ppermute | solution.py:20
  348.4 6.8 %collective-permute-start.5 = (f32[16,1,1536]{2,0,1:T(8,128)S(1)}, f32[16,1,1536]{2,0,1:T(8,128)S(1)}, u32[]{:S(2)}, u32[]{:S(2)}) collective-permute-start(f32[16,1,1536]{2,0,1:T(8,128)S(1)} %get-tuple-element.42), channel_id=1, source_target_pairs={{0,1},{1,2},{2,3},{3,4},{4,5},{5,6},{6,7},{7,8},{8,9},{9,10},{10,1... | collective-permute-start | bytes 294920 | tf_op jit(solution)/shard_map/ppermute | solution.py:17
  426.1 4.5 collective-permute-start.6
  428.1 6.8 %collective-permute-start.7 = (f32[16,1,1536]{2,0,1:T(8,128)S(1)}, f32[16,1,1536]{2,0,1:T(8,128)S(1)}, u32[]{:S(2)}, u32[]{:S(2)}) collective-permute-start(f32[16,1,1536]{2,0,1:T(8,128)S(1)} %get-tuple-element.40), channel_id=1, source_target_pairs={{0,1},{1,2},{2,3},{3,4},{4,5},{5,6},{6,7},{7,8},{8,9},{9,10},{10,1... | collective-permute-start | bytes 294920 | tf_op jit(solution)/shard_map/ppermute | solution.py:17
